TPU v7x, 128 devices: a whole 4x4x4 slice. The times are simulated.
128 devices in a mesh: row: 8 (over x, core), col: 16 (over y, z).
Axes of the slice: x: 4, y: 4, z: 4, core: 2. Of those that a mesh axis runs over, the one named last changes fastest.
Arguments:
- filtered: float32 [32768, 2048], P(('row', 'col')), as said below
- hamiltonian_applied: float32 [32768, 2048], P(('row', 'col')), as said below
- rotation: float32 [2048, 2048], replicated, may hold values from -0.125 to 0.125
Outputs:
- intersection: float32 [2048, 2048], P('row', 'col')
- projected: float32 [2048, 2048], P('row', 'col')
- rotated: float32 [32768, 2048], P(('row', 'col'))
Inputs may be any that keep to these rules, and one draw needn't show every extreme that they name: `filtered`: finite real values. `hamiltonian_applied`: finite real values.
All inputs are finite; a program needn't handle non-finite values.
Results may differ from a plain program's by a relative error of at most 0.00005.
Values sent between devices are 32-bit elements; how exact they have to be, the bound alone decides.
A program may use at most 192 MiB of HBM per device.

v0:
```python
import jax
import jax.numpy as jnp
from jax import lax
from jax.sharding import PartitionSpec as P


def inner_rows(first, second):
    return jnp.einsum(
        "gi,gj->ij",
        first,
        second,
        precision=lax.Precision.HIGHEST,
        preferred_element_type=jnp.float32,
    )


def product(first, second):
    return jnp.dot(
        first, second, precision=lax.Precision.HIGHEST, preferred_element_type=jnp.float32
    )


def local(filtered, hamiltonian_applied, rotation):
    cells = filtered.shape[0]
    col_count = lax.axis_size("col")
    row_count = lax.axis_size("row")
    scale = 1.0 / (cells * col_count * row_count)
    psi_band, ham_band = (
        lax.all_to_all(filtered, "col", split_axis=1, concat_axis=0, tiled=True),
        lax.all_to_all(hamiltonian_applied, "col", split_axis=1, concat_axis=0, tiled=True),
    )
    piece = lax.all_gather(psi_band, "col", axis=1, tiled=True)
    over_term = inner_rows(piece, psi_band) * scale
    proj_term = inner_rows(piece, ham_band) * scale
    over_term, proj_term = (over_term, proj_term)
    intersection, projected = (
        lax.psum_scatter(over_term, "row", scatter_dimension=0, tiled=True),
        lax.psum_scatter(proj_term, "row", scatter_dimension=0, tiled=True),
    )
    rotated = product(filtered, rotation)
    return (intersection, projected, rotated)


def solution(mesh):
    return jax.shard_map(
        local,
        mesh=mesh,
        in_specs=(P(("row", "col"), None), P(("row", "col"), None), P()),
        out_specs=(P("row", "col"), P("row", "col"), P(("row", "col"), None)),
        check_vma=False,
    )
```

profile of v0, /device:TPU:0, one launch (start us, length us, event | category | flops | bytes accessed | tf_op | source)
XLA Modules:
  0.0 426.3 jit_solution(1615125823483766629)
XLA Ops:
  7.2 0.0 all-gather.2.cloned.1.call-start
  7.2 2.9 copy.6
  10.1 36.4 %all_to_all.38 = f32[256,16,128]{0,2,1:T(8,128)S(1)} all-to-all(f32[256,16,128]{0,2,1:T(8,128)} %bitcast.17), channel_id=1, replica_groups=mesh['row'=8,'col'=16] {'col'}, dimensions={1} | all-to-all | bytes 4194304 | tf_op jit(solution)/shard_map/all_to_all | solution.py:29
  46.5 1.8 copy.7
  48.3 0.0 all-gather.2.cloned.1.call-update
  48.3 1.6 copy-done.2
  49.9 1.9 copy.8
  51.7 0.0 copy-start
  51.8 4.6 %all-to-all-start.1 = ((f32[256,16,128]{0,2,1:T(8,128)}), f32[256,16,128]{0,2,1:T(8,128)}, u32[]{:S(2)}, u32[]{:S(2)}) async-start(f32[256,16,128]{0,2,1:T(8,128)} %bitcast.15), calls=%async_computation.2 | async-start | bytes 4194304 | tf_op jit(solution)/shard_map/all_to_all | solution.py:30
  56.3 0.0 reduce-scatter.3.cloned.1.call-start
  56.4 215.1 %all-gather.2.cloned.1.call-done = f32[4096,2048]{1,0:T(8,128)} async-done(((f32[4096,128]{1,0:T(8,128)}), f32[4096,2048]{1,0:T(8,128)}) %all-gather.2.cloned.1.call-update) | async-done | bytes 33554448 | tf_op jit(solution)/shard_map/all_gather | solution.py:32
  271.5 0.0 copy-done
  271.5 56.6 %convolution_multiply_fusion.1 = f32[2048,128]{1,0:T(8,128)} fusion(f32[4096,2048]{1,0:T(8,128)} %all-gather.2.cloned.1.call-done, f32[4096,128]{1,0:T(8,128)S(1)} %bitcast.13), kind=kOutput, calls=%fused_computation.1 | convolution fusion | flops 12885164032 | bytes 36700160 | tf_op jit(solution)/shard_map/gi,gj->ij/dot_general | solution.py:8
  328.1 0.0 reduce-scatter.3.cloned.1.call-update
  328.1 0.0 reduce-scatter.5.cloned.1.call-start
  328.2 0.0 all-to-all-done.1
  328.2 2.9 copy.9
  331.1 0.0 copy-start.1
  331.1 57.4 %convolution_multiply_fusion = f32[2048,128]{1,0:T(8,128)} fusion(f32[4096,2048]{1,0:T(8,128)} %all-gather.2.cloned.1.call-done, f32[4096,128]{1,0:T(8,128)} %bitcast.14), kind=kOutput, calls=%fused_computation | convolution fusion | flops 12885164032 | bytes 36700160 | tf_op jit(solution)/shard_map/gi,gj->ij/dot_general | solution.py:8
  388.5 0.0 reduce-scatter.5.cloned.1.call-update
  388.5 0.0 copy-done.1
  388.5 17.8 %fusion = f32[256,2048]{1,0:T(8,128)} fusion(f32[256,2048]{1,0:T(8,128)S(1)} %copy-done.1, f32[2048,2048]{1,0:T(8,128)} %param.5), kind=kOutput, calls=%fused_computation.2 | convolution fusion | flops 12884901888 | bytes 20971520 | tf_op jit(solution)/shard_map/dot_general | solution.py:18
  406.3 0.0 reduce-scatter.3.cloned.1.call-done
  406.3 13.4 %reduce-scatter.5.cloned.1.call-done = f32[256,128]{1,0:T(8,128)} async-done(((f32[2048,128]{1,0:T(8,128)}), f32[256,128]{1,0:T(8,128)}) %reduce-scatter.5.cloned.1.call-update) | async-done | bytes 131088 | tf_op jit(solution)/shard_map/reduce_scatter | solution.py:38
  (1 shorter events, 0.0 us)
Async XLA Ops:
  7.2 264.3 %all-gather.2.cloned.1.call-start = ((), (), s32[]{:S(2)}) async-start(), calls=%async_computation.4 | async-start | bytes 35651584 | tf_op jit(solution)/shard_map/all_gather | solution.py:32
  48.3 1.6 copy-start.2
  51.7 219.7 %copy-start = (f32[16,256,128]{2,1,0:T(8,128)S(1)}, f32[16,256,128]{2,1,0:T(8,128)}, u32[]{:S(2)}) copy-start(f32[16,256,128]{2,1,0:T(8,128)} %copy.7) | copy-start | bytes 6291460
  51.8 276.4 %all-to-all-start.1 = ((f32[256,16,128]{0,2,1:T(8,128)}), f32[256,16,128]{0,2,1:T(8,128)}, u32[]{:S(2)}, u32[]{:S(2)}) async-start(f32[256,16,128]{0,2,1:T(8,128)} %bitcast.15), calls=%async_computation.2 | async-start | bytes 4194304 | tf_op jit(solution)/shard_map/all_to_all | solution.py:30
  56.3 350.0 %reduce-scatter.3.cloned.1.call-start = ((), (), s32[]{:S(2)}) async-start(), calls=%async_computation.5 | async-start | bytes 1179648 | tf_op jit(solution)/shard_map/reduce_scatter | solution.py:37
  328.1 91.6 %reduce-scatter.5.cloned.1.call-start = ((), (), s32[]{:S(2)}) async-start(), calls=%async_computation.6 | async-start | bytes 1179648 | tf_op jit(solution)/shard_map/reduce_scatter | solution.py:38
  331.1 57.4 %copy-start.1 = (f32[256,2048]{1,0:T(8,128)S(1)}, f32[256,2048]{1,0:T(8,128)}, u32[]{:S(2)}) copy-start(f32[256,2048]{1,0:T(8,128)} %param.3) | copy-start | bytes 6291460
Sparse Core Ops, SparseCore 0:
  48.4 223.0 all-gather.1
  328.3 31.0 reduce-scatter.2
  388.6 31.0 reduce-scatter.4
where the time goes:
time: 427 us; the launch traced here: 426 us
  waiting for transfers between devices  229 us (54%)
  matrix products  132 us (31%)
  blocking collectives  36.4 us (9%)
  between operations  13.8 us (3%)
  local copies, waits for them, and re-layouts  11 us (3%)
  starting transfers between devices  4.7 us (1%)
    all_gather x1, waiting for transfers between devices, local(): piece = lax.all_gather(psi_band, 'col', axis=1, tiled=True)  215 us
    dot_general x2, matrix products, inner_rows(): jnp.einsum('gi,gj->ij', first, second, precision=lax.Precision.HIGHEST, p...  114 us
    all_to_all x1, blocking collectives, local(): lax.all_to_all(filtered, 'col', split_axis=1, concat_axis=0, tiled=True)  36.4 us
    dot_general x1, matrix products, product(): jnp.dot(first, second, precision=lax.Precision.HIGHEST, preferred_element...  17.8 us
    reduce_scatter x1, waiting for transfers between devices, local(): lax.psum_scatter(proj_term, 'row', scatter_dimension=0, tiled=True)  13.4 us
  transfers between devices with their start and end apart: 4, of which 2 were waited for; matrix products, arithmetic and copies ran while one was open for 32% of the time, Pallas kernels for 0%

commit v1 on v0

--- a/solution.py
+++ b/solution.py
@@ -29,7 +29,9 @@
         lax.all_to_all(filtered, "col", split_axis=1, concat_axis=0, tiled=True),
         lax.all_to_all(hamiltonian_applied, "col", split_axis=1, concat_axis=0, tiled=True),
     )
-    piece = lax.all_gather(psi_band, "col", axis=1, tiled=True)
+    piece = jnp.concatenate(
+        lax.all_to_all(jnp.stack([psi_band] * lax.axis_size("col")), "col", 0, 0), axis=1
+    )
     over_term = inner_rows(piece, psi_band) * scale
     proj_term = inner_rows(piece, ham_band) * scale
     over_term, proj_term = (over_term, proj_term)

time: 427 us -> 795 us (1.86)
  waiting for transfers between devices: 229 us -> 623 us
  matrix products: 132 us -> 79.6 us
  starting transfers between devices: 4.7 us -> 17.5 us
  local copies, waits for them, and re-layouts: 11 us -> 23.6 us
    all_to_all x0 -> x1, waiting for transfers between devices: none -> 607 us  [local(): lax.all_to_all(jnp.stack([psi_band] * lax.axis_size('col')), 'col', 0, 0)]
    all_gather x1 -> x0, waiting for transfers between devices: 215 us -> none  [local(): piece = lax.all_gather(psi_band, 'col', axis=1, tiled=True)]
    dot_general x2, matrix products: 114 us -> 61.9 us  [inner_rows(): jnp.einsum('gi,gj->ij', first, second, precision=lax.Precision.HIGHEST, p...]
    another operation x0 -> x2, local copies, waits for them, and re-layouts: none -> 14 us  [local(): jnp.stack([psi_band] * lax.axis_size('col'))]
  transfers between devices with their start and end apart: 4 -> 4, of which waited for: 2 -> 2; matrix products, arithmetic and copies ran while one was open for 32% -> 11% of each run, Pallas kernels for 0% -> 0%
where the time goes in v1:
time: 795 us; the launch traced here: 794 us
  waiting for transfers between devices  623 us (78%)
  matrix products  79.6 us (10%)
  blocking collectives  36.3 us (5%)
  local copies, waits for them, and re-layouts  23.6 us (3%)
  starting transfers between devices  17.5 us (2%)
  between operations  14.1 us (2%)
    all_to_all x1, waiting for transfers between devices, local(): lax.all_to_all(jnp.stack([psi_band] * lax.axis_size('col')), 'col', 0, 0)  607 us
    dot_general x2, matrix products, inner_rows(): jnp.einsum('gi,gj->ij', first, second, precision=lax.Precision.HIGHEST, p...  61.9 us
    all_to_all x1, blocking collectives, local(): lax.all_to_all(filtered, 'col', split_axis=1, concat_axis=0, tiled=True)  36.3 us
    dot_general x1, matrix products, product(): jnp.dot(first, second, precision=lax.Precision.HIGHEST, preferred_element...  17.8 us
  transfers between devices with their start and end apart: 4, of which 2 were waited for; matrix products, arithmetic and copies ran while one was open for 11% of the time, Pallas kernels for 0%

profile of v1, /device:TPU:0, one launch (start us, length us, event | category | flops | bytes accessed | tf_op | source)
XLA Modules:
  0.0 794.3 jit_solution(493579519644329692)
XLA Ops:
  7.2 1.9 copy.7
  9.1 36.3 %all_to_all.40 = f32[256,16,128]{0,2,1:T(8,128)} all-to-all(f32[256,16,128]{0,2,1:T(8,128)S(1)} %bitcast.20), channel_id=1, replica_groups=mesh['row'=8,'col'=16] {'col'}, dimensions={1} | all-to-all | bytes 4194304 | tf_op jit(solution)/shard_map/all_to_all | solution.py:29
  45.4 1.9 copy.8
  47.3 1.8 copy.9
  49.1 12.2 %stack.5 = f32[16,4096,128]{1,2,0:T(8,128)} broadcast(f32[4096,128]{0,1:T(8,128)} %copy.9), dimensions={1,2} | broadcast | bytes 35651584 | tf_op jit(solution)/shard_map/stack | solution.py:33
  61.3 5.9 all-to-all-start.1
  67.2 2.9 copy.10
  70.1 607.5 %all-to-all-done.1 = f32[16,4096,128]{1,2,0:T(8,128)} async-done(((f32[16,4096,128]{1,2,0:T(8,128)}), f32[16,4096,128]{1,2,0:T(8,128)}, u32[]{:S(2)}, u32[]{:S(2)}) %all-to-all-start.1) | async-done | bytes 33554464 | tf_op jit(solution)/shard_map/all_to_all | solution.py:33
  677.6 11.3 %all-to-all-start.2 = ((f32[256,16,128]{0,2,1:T(8,128)}), f32[256,16,128]{0,2,1:T(8,128)}, u32[]{:S(2)}, u32[]{:S(2)}) async-start(f32[256,16,128]{0,2,1:T(8,128)} %bitcast.18), calls=%async_computation.3 | async-start | bytes 4194304 | tf_op jit(solution)/shard_map/all_to_all | solution.py:30
  688.9 0.0 reduce-scatter.3.cloned.1.call-start
  688.9 30.8 %convolution_multiply_fusion.1 = f32[2048,128]{1,0:T(8,128)} fusion(f32[4096,2048]{0,1:T(8,128)} %bitcast.4, f32[4096,128]{1,0:T(8,128)S(1)} %bitcast.16), kind=kOutput, calls=%fused_computation.1 | convolution fusion | flops 12885164032 | bytes 36700160 | tf_op jit(solution)/shard_map/gi,gj->ij/dot_general | solution.py:8
  719.7 0.0 reduce-scatter.3.cloned.1.call-update
  719.7 0.2 reduce-scatter.5.cloned.1.call-start
  719.9 0.0 all-to-all-done.2
  720.0 2.9 copy.11
  722.8 0.0 copy-start
  722.8 31.1 %convolution_multiply_fusion = f32[2048,128]{1,0:T(8,128)} fusion(f32[4096,2048]{0,1:T(8,128)} %bitcast.4, f32[4096,128]{1,0:T(8,128)} %bitcast.17), kind=kOutput, calls=%fused_computation | convolution fusion | flops 12885164032 | bytes 36700160 | tf_op jit(solution)/shard_map/gi,gj->ij/dot_general | solution.py:8
  753.9 0.0 reduce-scatter.5.cloned.1.call-update
  754.0 0.0 copy-done
  754.0 17.8 %fusion = f32[256,2048]{1,0:T(8,128)} fusion(f32[256,2048]{1,0:T(8,128)S(1)} %copy-done, f32[2048,2048]{1,0:T(8,128)} %param.5), kind=kOutput, calls=%fused_computation.2 | convolution fusion | flops 12884901888 | bytes 20971520 | tf_op jit(solution)/shard_map/dot_general | solution.py:18
  771.7 0.0 reduce-scatter.3.cloned.1.call-done
  771.7 15.7 %reduce-scatter.5.cloned.1.call-done = f32[256,128]{1,0:T(8,128)} async-done(((f32[2048,128]{1,0:T(8,128)}), f32[256,128]{1,0:T(8,128)}) %reduce-scatter.5.cloned.1.call-update) | async-done | bytes 131088 | tf_op jit(solution)/shard_map/reduce_scatter | solution.py:40
Async XLA Ops:
  61.3 616.3 %all-to-all-start.1 = ((f32[16,4096,128]{1,2,0:T(8,128)}), f32[16,4096,128]{1,2,0:T(8,128)}, u32[]{:S(2)}, u32[]{:S(2)}) async-start(f32[16,4096,128]{1,2,0:T(8,128)} %stack.5), calls=%async_computation.1 | async-start | bytes 67108864 | tf_op jit(solution)/shard_map/all_to_all | solution.py:33
  677.6 42.4 %all-to-all-start.2 = ((f32[256,16,128]{0,2,1:T(8,128)}), f32[256,16,128]{0,2,1:T(8,128)}, u32[]{:S(2)}, u32[]{:S(2)}) async-start(f32[256,16,128]{0,2,1:T(8,128)} %bitcast.18), calls=%async_computation.3 | async-start | bytes 4194304 | tf_op jit(solution)/shard_map/all_to_all | solution.py:30
  688.9 82.9 %reduce-scatter.3.cloned.1.call-start = ((), (), s32[]{:S(2)}) async-start(), calls=%async_computation.5 | async-start | bytes 1179648 | tf_op jit(solution)/shard_map/reduce_scatter | solution.py:39
  719.7 67.7 %reduce-scatter.5.cloned.1.call-start = ((), (), s32[]{:S(2)}) async-start(), calls=%async_computation.6 | async-start | bytes 1179648 | tf_op jit(solution)/shard_map/reduce_scatter | solution.py:40
  722.8 31.1 %copy-start = (f32[256,2048]{1,0:T(8,128)S(1)}, f32[256,2048]{1,0:T(8,128)}, u32[]{:S(2)}) copy-start(f32[256,2048]{1,0:T(8,128)} %param.3) | copy-start | bytes 6291460
Sparse Core Ops, SparseCore 0:
  719.8 33.3 reduce-scatter.2
  756.2 31.2 reduce-scatter.4
